TPU v7x, 32 devices: a whole 2x2x4 slice. The times are simulated.
32 devices in a mesh: ctx: 8 (over z, x), head: 4 (over y, core).
Axes of the slice: x: 2, y: 2, z: 4, core: 2. Of those that a mesh axis runs over, the one named last changes fastest.
Arguments:
- hidden: bfloat16 [256, 8192], P(None, 'ctx')
- norm_gain: float32 [8192], replicated, may hold values from 0.1 to 1.9
- w_query: bfloat16 [8192, 8192], P('ctx', 'head'), may hold values from -0.0625 to 0.0625
- manifest_keys: bfloat16 [8, 4096, 128], P(None, 'ctx')
- manifest_values: bfloat16 [8, 4096, 128], P(None, 'ctx'), may hold values from -6 to 6
- w_output: bfloat16 [8192, 8192], P('head', 'ctx'), may hold values from -0.0625 to 0.0625
- valid_len: int32 [256], replicated, may hold values from 1 to 4096, as said below
- home_block: int32 [256], replicated, may hold values from 0 to 7, as said below
Outputs:
- projected: float32 [256, 8192], P('head', 'ctx')
Inputs may be any that keep to these rules, and one draw needn't show every extreme that they name: `valid_len`: every draw has a row that reads the whole manifest and a row with length 1. `home_block`: every draw assigns some row to the first block and some row to the last.
All inputs are finite; a program needn't handle non-finite values.
Results may differ from a plain program's by a relative error of at most 0.005.
The roundings to bfloat16 on the way count: a program that leaves them out, or rounds other values in their place, can miss the bound.
Values may be sent and summed in bfloat16 or wider, within the bound.
A program may use at most 128 MiB of HBM per device.

v0:
```python
import math
import jax
import jax.numpy as jnp
from jax import lax
from jax.sharding import PartitionSpec as P

H = 64
KVH = 8
HD = 128


def shards(
    hidden, norm_gain, w_query, manifest_keys, manifest_values, w_output, valid_len, home_block
):
    ctx_count = lax.axis_size("ctx")
    ctx_index = lax.axis_index("ctx")
    head_index = lax.axis_index("head")
    rows, feat = hidden.shape
    d_model = feat * ctx_count
    width = w_query.shape[1]
    heads_here = width // HD
    group = H // KVH
    span = manifest_keys.shape[1]
    hsplit = min(ctx_count, heads_here)
    rsplit = ctx_count // hsplit
    rows_dev = rows // rsplit
    heads_dev = heads_here // hsplit
    widened = hidden.astype(jnp.float32)
    total_sq = lax.psum(jnp.sum(widened * widened, axis=1, keepdims=True), "ctx")
    inv_rms = lax.rsqrt(total_sq / d_model + 1e-05)
    gain = lax.dynamic_slice_in_dim(norm_gain, ctx_index * feat, feat, 0)
    normed = (widened * inv_rms * gain[None, :]).astype(jnp.bfloat16)
    partial = jnp.dot(normed, w_query, preferred_element_type=jnp.float32)
    partial = partial.reshape(rsplit, rows_dev, hsplit, heads_dev * HD).transpose(2, 0, 1, 3)
    partial = partial.reshape(ctx_count, rows_dev, heads_dev * HD)
    query = lax.psum_scatter(partial, "ctx", scatter_dimension=0, tiled=False).astype(jnp.bfloat16)
    dest_heads = head_index * heads_here + jnp.arange(ctx_count) // rsplit * heads_dev
    dest_kv = dest_heads // group
    kv = jnp.stack([manifest_keys[dest_kv], manifest_values[dest_kv]], axis=1)
    kv = lax.all_to_all(kv, "ctx", split_axis=0, concat_axis=0, tiled=True)
    kv = kv.transpose(1, 0, 2, 3).reshape(2, ctx_count * span, HD)
    keys, values = (kv[0], kv[1])
    first_row = ctx_index % rsplit * rows_dev
    lens = lax.dynamic_slice_in_dim(valid_len, first_row, rows_dev, 0)
    blocks = lax.dynamic_slice_in_dim(home_block, first_row, rows_dev, 0)
    places = jnp.arange(ctx_count * span, dtype=jnp.int32)
    usable = (places[None, :] < lens[:, None]) | ((places // span)[None, :] == blocks[:, None])
    usable = usable[:, None, :]
    q3 = query.reshape(rows_dev, heads_dev, HD)
    scores = jnp.einsum("nhd,jd->nhj", q3, keys, preferred_element_type=jnp.float32) * (
        1.0 / math.sqrt(HD)
    )
    scores = jnp.where(usable, scores, -1e30)
    row_max = jnp.max(scores, axis=2, keepdims=True)
    expo = jnp.where(usable, jnp.exp(scores - row_max), 0.0)
    row_sum = jnp.sum(expo, axis=2, keepdims=True)
    weighted = jnp.einsum(
        "nhj,jd->nhd", expo.astype(jnp.bfloat16), values, preferred_element_type=jnp.float32
    )
    attn = (weighted / row_sum).astype(jnp.bfloat16).reshape(rows_dev, heads_dev * HD)
    attn = lax.all_gather(attn, "ctx", axis=0, tiled=False)
    attn = attn.reshape(hsplit, rsplit, rows_dev, heads_dev * HD).transpose(1, 2, 0, 3)
    attn = attn.reshape(rows, width)
    return lax.psum_scatter(
        jnp.dot(attn, w_output, preferred_element_type=jnp.float32),
        "head",
        scatter_dimension=0,
        tiled=True,
    )


def solution(mesh):
    in_specs = (
        P(None, "ctx"),
        P(),
        P("ctx", "head"),
        P(None, "ctx", None),
        P(None, "ctx", None),
        P("head", "ctx"),
        P(),
        P(),
    )
    out_specs = P("head", "ctx")
    return jax.shard_map(shards, mesh=mesh, in_specs=in_specs, out_specs=out_specs, check_vma=False)
```

profile of v0, /device:TPU:0, one launch (start us, length us, event | category | flops | bytes accessed | tf_op | source)
XLA Modules:
  0.0 222.7 jit_solution(15778530597544170264)
XLA Ops:
  6.5 0.0 copy-start
  6.5 0.0 reduce-scatter.3.cloned.1.call-start
  6.5 1.3 fusion.14
  7.9 23.1 %psum.7 = f32[256,1]{0,1:T(1,128)S(1)} all-reduce(f32[256,1]{0,1:T(1,128)S(1)} %bitcast.42), channel_id=1, replica_groups=mesh['ctx'=8,'head'=4] {'ctx'}, use_global_device_ids=true, to_apply=%region_1.0 | all-reduce | flops 256 | bytes 2048 | tf_op jit(solution)/shard_map/psum | solution.py:29
  31.0 0.7 dynamic_slice.2
  31.6 5.5 %fusion.19 = f32[256,2048]{0,1:T(8,128)} fusion(bf16[1024,2048]{1,0:T(8,128)(2,1)} %param.10, bf16[256,1024]{1,0:T(8,128)(2,1)} %param.8, f32[1024]{0:T(1024)S(1)} %dynamic_slice.2, f32[256]{0:T(256)S(1)} %bitcast.43), kind=kOutput, calls=%fused_computation.22 | convolution fusion | flops 1074790400 | bytes 6820864 | tf_op jit(solution)/shard_map/reshape | solution.py:34
  37.2 0.0 reduce-scatter.3.cloned.1.call-update
  37.2 0.0 copy-done
  37.2 0.7 gather_fusion.1
  38.0 2.0 gather_fusion
  40.0 0.0 copy-start.2
  40.0 0.0 copy-start.3
  40.0 1.5 pad_maximum_fusion
  41.5 3.6 %all-to-all-start = ((bf16[8,2,512,128]{3,2,1,0:T(8,128)(2,1)}), bf16[8,2,512,128]{3,2,1,0:T(8,128)(2,1)S(1)}, u32[]{:S(2)}, u32[]{:S(2)}) async-start(bf16[8,2,512,128]{3,2,1,0:T(8,128)(2,1)} %pad_maximum_fusion), calls=%async_computation.1 | async-start | bytes 4194304 | tf_op jit(solution)/shard_map/all_to_all | solution.py:40
  45.1 0.0 all-gather.2.cloned.1.call-start
  45.1 0.0 copy-done.2
  45.2 0.0 copy-done.3
  45.2 1.9 fusion.6
  47.0 59.5 %all-to-all-done = bf16[8,2,512,128]{3,2,1,0:T(8,128)(2,1)S(1)} async-done(((bf16[8,2,512,128]{3,2,1,0:T(8,128)(2,1)}), bf16[8,2,512,128]{3,2,1,0:T(8,128)(2,1)S(1)}, u32[]{:S(2)}, u32[]{:S(2)}) %all-to-all-start) | async-done | bytes 2097184 | tf_op jit(solution)/shard_map/all_to_all | solution.py:40
  106.5 1.5 fusion.29
  108.0 25.2 %reduce-scatter.3.cloned.1.call-done = f32[1,256,256]{1,2,0:T(8,128)} async-done(((f32[8,256,256]{1,2,0:T(8,128)}), f32[1,256,256]{1,2,0:T(8,128)}) %reduce-scatter.3.cloned.1.call-update) | async-done | bytes 262160 | tf_op jit(solution)/shard_map/reduce_scatter | solution.py:36
  133.2 1.0 convert_element_type.21
  134.2 0.0 copy-start.1
  134.2 8.3 %fusion.30 = (f32[256,2]{0,1:T(2,128)S(1)}, bf16[256,2,4096]{2,0,1:T(8,128)(2,1)}) fusion(pred[256,4096]{1,0:T(8,128)(4,1)} %fusion.6, bf16[256,2,128]{0,2,1:T(8,128)(2,1)S(1)} %bitcast.41, bf16[4096,128,1]{1,0,2:T(8,128)(2,1)} %bitcast.39), kind=kOutput, calls=%fused_computation.43 | convolution fusion | flops 549457920 | bytes 6424576 | tf_op jit(solution)/shard_map/sub | solution.py:55
  142.5 0.0 copy-done.1
  142.5 3.7 %fusion.11 = bf16[256,2,128]{0,2,1:T(8,128)(2,1)S(1)} fusion(bf16[4096,128,1]{1,0,2:T(8,128)(2,1)S(1)} %bitcast.34, bf16[256,2,4096]{2,0,1:T(8,128)(2,1)} %get-tuple-element.8, f32[256,2]{0,1:T(2,128)S(1)} %get-tuple-element.7), kind=kOutput, calls=%fused_computation.17 | convolution fusion | flops 537001984 | bytes 5376000 | tf_op jit(solution)/shard_map/nhj,jd->nhd/dot_general | solution.py:57
  146.2 0.8 copy.20
  146.9 0.0 all-gather.2.cloned.1.call-update
  147.0 0.0 reduce-scatter.5.cloned.1.call-start
  147.0 39.4 %all-gather.2.cloned.1.call-done = bf16[8,256,256]{2,1,0:T(8,128)(2,1)} async-done(((bf16[1,256,256]{2,1,0:T(8,128)(2,1)}), bf16[8,256,256]{2,1,0:T(8,128)(2,1)}) %all-gather.2.cloned.1.call-update) | async-done | bytes 1048592 | tf_op jit(solution)/shard_map/all_gather | solution.py:61
  186.4 1.5 copy.21
  187.9 4.5 %fusion.31 = f32[256,1024]{1,0:T(8,128)} fusion(bf16[256,2048]{0,1:T(8,128)(2,1)S(1)} %bitcast.38, bf16[2048,1024]{1,0:T(8,128)(2,1)} %param.13), kind=kOutput, calls=%fused_computation.44 | convolution fusion | flops 1073741824 | bytes 6291456 | tf_op jit(solution)/shard_map/dot_general | solution.py:65
  192.4 0.0 reduce-scatter.5.cloned.1.call-update
  192.4 23.8 %reduce-scatter.5.cloned.1.call-done = f32[64,1024]{1,0:T(8,128)} async-done(((f32[256,1024]{1,0:T(8,128)}), f32[64,1024]{1,0:T(8,128)}) %reduce-scatter.5.cloned.1.call-update) | async-done | bytes 262160 | tf_op jit(solution)/shard_map/reduce_scatter | solution.py:64
  (4 shorter events, 0.0 us)
Async XLA Ops:
  6.5 30.7 %copy-start = (bf16[8,512,128]{2,1,0:T(8,128)(2,1)S(1)}, bf16[8,512,128]{2,1,0:T(8,128)(2,1)}, u32[]{:S(2)}) copy-start(bf16[8,512,128]{2,1,0:T(8,128)(2,1)} %param.12) | copy-start | bytes 3145732
  6.5 126.7 %reduce-scatter.3.cloned.1.call-start = ((), (), s32[]{:S(2)}) async-start(), calls=%async_computation.3 | async-start | bytes 2359296 | tf_op jit(solution)/shard_map/reduce_scatter | solution.py:36
  40.0 5.2 %copy-start.2 = (s32[256]{0:T(256)S(1)}, s32[256]{0:T(256)}, u32[]{:S(2)}) copy-start(s32[256]{0:T(256)} %param.14) | copy-start | bytes 3076
  40.0 5.2 %copy-start.3 = (s32[256]{0:T(256)S(1)}, s32[256]{0:T(256)}, u32[]{:S(2)}) copy-start(s32[256]{0:T(256)} %param.15) | copy-start | bytes 3076
  41.5 65.0 %all-to-all-start = ((bf16[8,2,512,128]{3,2,1,0:T(8,128)(2,1)}), bf16[8,2,512,128]{3,2,1,0:T(8,128)(2,1)S(1)}, u32[]{:S(2)}, u32[]{:S(2)}) async-start(bf16[8,2,512,128]{3,2,1,0:T(8,128)(2,1)} %pad_maximum_fusion), calls=%async_computation.1 | async-start | bytes 4194304 | tf_op jit(solution)/shard_map/all_to_all | solution.py:40
  45.1 141.3 %all-gather.2.cloned.1.call-start = ((), (), s32[]{:S(2)}) async-start(), calls=%async_computation.4 | async-start | bytes 1179648 | tf_op jit(solution)/shard_map/all_gather | solution.py:61
  134.2 8.3 %copy-start.1 = (bf16[1,8,512,128]{3,2,0,1:T(8,128)(2,1)S(1)}, bf16[1,8,512,128]{3,2,0,1:T(8,128)(2,1)}, u32[]{:S(2)}) copy-start(bf16[1,8,512,128]{3,2,0,1:T(8,128)(2,1)} %get-tuple-element.6) | copy-start | bytes 3145732
  147.0 69.2 %reduce-scatter.5.cloned.1.call-start = ((), (), s32[]{:S(2)}) async-start(), calls=%async_computation.5 | async-start | bytes 1310720 | tf_op jit(solution)/shard_map/reduce_scatter | solution.py:64
Sparse Core Ops, SparseCore 0:
  37.3 95.8 reduce-scatter.2
  147.1 39.2 all-gather.1
  192.5 23.6 reduce-scatter.4
where the time goes:
time: 223 us
  waiting for transfers between devices  148 us (66%)
  blocking collectives  23.1 us (10%)
  matrix products  22 us (10%)
  between operations  13.2 us (6%)
  local copies, waits for them, and re-layouts  7.19 us (3%)
  other arithmetic  5.66 us (3%)
  starting transfers between devices  3.69 us (2%)
    all_to_all x1, waiting for transfers between devices, shards(): kv = lax.all_to_all(kv, 'ctx', split_axis=0, concat_axis=0, tiled=True)  59.5 us
    all_gather x1, waiting for transfers between devices, shards(): attn = lax.all_gather(attn, 'ctx', axis=0, tiled=False)  39.4 us
    reduce_scatter x1, waiting for transfers between devices, shards(): lax.psum_scatter(partial, 'ctx', scatter_dimension=0, tiled=False)  25.2 us
    reduce_scatter x1, waiting for transfers between devices, shards(): lax.psum_scatter(jnp.dot(attn, w_output, preferred_element_type=jnp.float...  23.8 us
    psum x1, blocking collectives, shards(): lax.psum(jnp.sum(widened * widened, axis=1, keepdims=True), 'ctx')  23.1 us
    sub x1, matrix products, shards(): expo = jnp.where(usable, jnp.exp(scores - row_max), 0.0)  8.3 us
    reshape x1, matrix products, shards(): partial.reshape(rsplit, rows_dev, hsplit, heads_dev * HD)  5.51 us
    dot_general x1, matrix products, shards(): jnp.dot(attn, w_output, preferred_element_type=jnp.float32)  4.46 us
  transfers between devices with their start and end apart: 4, of which 4 were waited for; matrix products, arithmetic and copies ran while one was open for 3% of the time, Pallas kernels for 0%

commit v1 on v0

--- a/solution.py
+++ b/solution.py
@@ -3,15 +3,46 @@
 import jax.numpy as jnp
 from jax import lax
 from jax.sharding import PartitionSpec as P
+from jax.lax import axis_index, ppermute, psum
 
 H = 64
 KVH = 8
 HD = 128
 
 
+def do_the_surface(message, ndim_at, x_in):
+    f_now = message.shape
+    passed = message.reshape(*f_now[:ndim_at], x_in, f_now[ndim_at] // x_in, *f_now[ndim_at + 1 :])
+    odd = jnp.moveaxis(passed, ndim_at, 0)
+    return odd
+
+
+def _launch_sides(state, out_dim):
+    state = jnp.moveaxis(state, 0, out_dim)
+    r2 = state.shape
+    upper = state.reshape(*r2[:out_dim], r2[out_dim] * r2[out_dim + 1], *r2[out_dim + 2 :])
+    return upper
+
+
 def shards(
     hidden, norm_gain, w_query, manifest_keys, manifest_values, w_output, valid_len, home_block
 ):
+
+    def _convert_tracks(net_axis, incoming_x, local_values, work_x=0):
+        part_next = psum(1, net_axis)
+        raw_out = axis_index(net_axis)
+        side_arr, view_out = (part_next, raw_out)
+        val = do_the_surface(local_values, incoming_x, side_arr)
+        history = [val[view_out]]
+        for dev_i in range(1, side_arr):
+            state_now = val[view_out ^ dev_i]
+            last = ppermute(state_now, net_axis, perm=[(d, d ^ dev_i) for d in range(side_arr)])
+            history.append(last)
+        block_now = jnp.stack(history, axis=0)
+        val = block_now[view_out ^ jnp.arange(side_arr)]
+        local_next = _launch_sides(val, work_x)
+        return local_next
+
     ctx_count = lax.axis_size("ctx")
     ctx_index = lax.axis_index("ctx")
     head_index = lax.axis_index("head")
@@ -37,7 +68,7 @@
     dest_heads = head_index * heads_here + jnp.arange(ctx_count) // rsplit * heads_dev
     dest_kv = dest_heads // group
     kv = jnp.stack([manifest_keys[dest_kv], manifest_values[dest_kv]], axis=1)
-    kv = lax.all_to_all(kv, "ctx", split_axis=0, concat_axis=0, tiled=True)
+    kv = _convert_tracks("ctx", 0, kv)
     kv = kv.transpose(1, 0, 2, 3).reshape(2, ctx_count * span, HD)
     keys, values = (kv[0], kv[1])
     first_row = ctx_index % rsplit * rows_dev

time: 223 us -> 216 us (0.969)
  waiting for transfers between devices: 148 us -> 129 us
  local copies, waits for them, and re-layouts: 7.19 us -> 16 us
  starting transfers between devices: 3.69 us -> 6.85 us
    all_to_all x1 -> x0, waiting for transfers between devices: 59.5 us -> none  [shards(): kv = lax.all_to_all(kv, 'ctx', split_axis=0, concat_axis=0, tiled=True)]
    ppermute x0 -> x7, waiting for transfers between devices: none -> 44.2 us  [_convert_tracks(): ppermute(state_now, net_axis, perm=[(d, d ^ dev_i) for d in range(side_ar...]
    ppermute x0 -> x7, starting transfers between devices: none -> 6.77 us  [_convert_tracks(): ppermute(state_now, net_axis, perm=[(d, d ^ dev_i) for d in range(side_ar...]
    unnamed x8 -> x20, local copies, waits for them, and re-layouts: 0.02 us -> 5.34 us
    reduce_scatter x1, waiting for transfers between devices: 25.2 us -> 21.3 us  [shards(): lax.psum_scatter(partial, 'ctx', scatter_dimension=0, tiled=False)]
    all_to_all x1 -> x0, starting transfers between devices: 3.6 us -> none  [shards(): kv = lax.all_to_all(kv, 'ctx', split_axis=0, concat_axis=0, tiled=True)]
    gather x0 -> x1, local copies, waits for them, and re-layouts: none -> 2.55 us  [_convert_tracks(): val = block_now[view_out ^ jnp.arange(side_arr)]]
  transfers between devices with their start and end apart: 4 -> 10, of which waited for: 4 -> 8; matrix products, arithmetic and copies ran while one was open for 3% -> 7% of each run, Pallas kernels for 0% -> 0%
where the time goes in v1:
time: 216 us; the launch traced here: 215 us
  waiting for transfers between devices  129 us (60%)
  blocking collectives  23.1 us (11%)
  matrix products  21.9 us (10%)
  local copies, waits for them, and re-layouts  16 us (7%)
  between operations  13.3 us (6%)
  starting transfers between devices  6.85 us (3%)
  other arithmetic  5.41 us (3%)
    ppermute x7, waiting for transfers between devices, _convert_tracks(): ppermute(state_now, net_axis, perm=[(d, d ^ dev_i) for d in range(side_ar...  44.2 us
    all_gather x1, waiting for transfers between devices, shards(): attn = lax.all_gather(attn, 'ctx', axis=0, tiled=False)  39.4 us
    reduce_scatter x1, waiting for transfers between devices, shards(): lax.psum_scatter(jnp.dot(attn, w_output, preferred_element_type=jnp.float...  23.8 us
    psum x1, blocking collectives, shards(): lax.psum(jnp.sum(widened * widened, axis=1, keepdims=True), 'ctx')  23.1 us
    reduce_scatter x1, waiting for transfers between devices, shards(): lax.psum_scatter(partial, 'ctx', scatter_dimension=0, tiled=False)  21.3 us
    sub x1, matrix products, shards(): expo = jnp.where(usable, jnp.exp(scores - row_max), 0.0)  8.31 us
    ppermute x7, starting transfers between devices, _convert_tracks(): ppermute(state_now, net_axis, perm=[(d, d ^ dev_i) for d in range(side_ar...  6.77 us
    reshape x1, matrix products, shards(): partial.reshape(rsplit, rows_dev, hsplit, heads_dev * HD)  5.5 us
  transfers between devices with their start and end apart: 10, of which 8 were waited for; matrix products, arithmetic and copies ran while one was open for 7% of the time, Pallas kernels for 0%

profile of v1, /device:TPU:0, one launch (start us, length us, event | category | flops | bytes accessed | tf_op | source)
XLA Modules:
  0.0 215.4 jit_solution(11695583335263270909)
XLA Ops:
  6.5 0.0 copy-start
  6.5 0.0 reduce-scatter.3.cloned.1.call-start
  6.5 1.3 fusion.14
  7.9 23.1 %psum.7 = f32[256,1]{0,1:T(1,128)S(1)} all-reduce(f32[256,1]{0,1:T(1,128)S(1)} %bitcast.78), channel_id=1, replica_groups=mesh['ctx'=8,'head'=4] {'ctx'}, use_global_device_ids=true, to_apply=%region_1.0 | all-reduce | flops 256 | bytes 2048 | tf_op jit(solution)/shard_map/psum | solution.py:60
  31.0 0.7 dynamic_slice.4
  31.6 5.5 %fusion.19 = f32[256,2048]{0,1:T(8,128)} fusion(bf16[1024,2048]{1,0:T(8,128)(2,1)} %param.10, bf16[256,1024]{1,0:T(8,128)(2,1)} %param.8, f32[1024]{0:T(1024)S(1)} %dynamic_slice.4, f32[256]{0:T(256)S(1)} %bitcast.79), kind=kOutput, calls=%fused_computation.38 | convolution fusion | flops 1074790400 | bytes 6820864 | tf_op jit(solution)/shard_map/reshape | solution.py:65
  37.2 0.0 reduce-scatter.3.cloned.1.call-update
  37.2 0.0 all-gather.2.cloned.1.call-start
  37.3 0.0 copy-done
  37.3 0.7 gather_fusion.1
  38.0 2.0 gather_fusion
  40.1 0.0 copy-start.5
  40.1 0.0 copy-start.6
  40.1 0.1 collective-permute-start.5
  40.2 1.2 fusion.23
  41.4 1.0 collective-permute-start.6
  42.4 4.2 %collective-permute-start = (bf16[1,2,512,128]{3,2,1,0:T(8,128)(2,1)}, bf16[1,2,512,128]{3,2,1,0:T(8,128)(2,1)}, u32[]{:S(2)}, u32[]{:S(2)}) collective-permute-start(bf16[1,2,512,128]{3,2,1,0:T(8,128)(2,1)} %get-tuple-element.8), channel_id=1, source_target_pairs={{0,4},{4,0},{8,12},{12,8},{16,20},{20,16},{24,28},{28,24},{1,5},{5... | collective-permute-start | bytes 786440 | tf_op jit(solution)/shard_map/ppermute | solution.py:39
  46.6 0.0 collective-permute-start.1
  46.6 1.5 collective-permute-start.2
  48.1 0.0 copy-done.5
  48.1 0.0 copy-done.6
  48.1 1.9 fusion.6
  50.0 0.0 copy-start.4
  50.0 0.0 copy-start.3
  50.0 6.9 %collective-permute-done = bf16[1,2,512,128]{3,2,1,0:T(8,128)(2,1)} collective-permute-done((bf16[1,2,512,128]{3,2,1,0:T(8,128)(2,1)}, bf16[1,2,512,128]{3,2,1,0:T(8,128)(2,1)}, u32[]{:S(2)}, u32[]{:S(2)}) %collective-permute-start) | collective-permute-done | bytes 262176 | tf_op jit(solution)/shard_map/ppermute | solution.py:39
  57.0 0.0 copy-done.4
  57.0 0.0 collective-permute-start.3
  57.0 1.0 bitcast_dynamic-update-slice_fusion.6
  57.9 16.1 %collective-permute-done.1 = bf16[1,2,512,128]{3,2,1,0:T(8,128)(2,1)} collective-permute-done((bf16[1,2,512,128]{3,2,1,0:T(8,128)(2,1)}, bf16[1,2,512,128]{3,2,1,0:T(8,128)(2,1)}, u32[]{:S(2)}, u32[]{:S(2)}) %collective-permute-start.1) | collective-permute-done | bytes 262176 | tf_op jit(solution)/shard_map/ppermute | solution.py:39
  74.0 0.0 copy-done.3
  74.0 0.0 collective-permute-start.4
  74.0 1.0 bitcast_dynamic-update-slice_fusion.5
  75.0 9.3 %collective-permute-done.2 = bf16[1,2,512,128]{3,2,1,0:T(8,128)(2,1)} collective-permute-done((bf16[1,2,512,128]{3,2,1,0:T(8,128)(2,1)}, bf16[1,2,512,128]{3,2,1,0:T(8,128)(2,1)}, u32[]{:S(2)}, u32[]{:S(2)}) %collective-permute-start.2) | collective-permute-done | bytes 262176 | tf_op jit(solution)/shard_map/ppermute | solution.py:39
  84.3 1.0 bitcast_dynamic-update-slice_fusion.4
  85.3 10.9 %collective-permute-done.3 = bf16[1,2,512,128]{3,2,1,0:T(8,128)(2,1)S(1)} collective-permute-done((bf16[1,2,512,128]{3,2,1,0:T(8,128)(2,1)S(1)}, bf16[1,2,512,128]{3,2,1,0:T(8,128)(2,1)S(1)}, u32[]{:S(2)}, u32[]{:S(2)}) %collective-permute-start.3) | collective-permute-done | bytes 262176 | tf_op jit(solution)/shard_map/ppermute | solution.py:39
  96.2 1.0 collective-permute-done.4
  97.2 0.0 collective-permute-done.5
  97.3 1.0 bitcast_dynamic-update-slice_fusion.1
  98.2 0.0 collective-permute-done.6
  98.3 1.0 bitcast_dynamic-update-slice_fusion
  99.2 0.0 copy-start.2
  99.3 1.3 copy-done.2
  100.6 2.5 %gather_fusion.2 = bf16[8,2,512,128]{3,2,1,0:T(8,128)(2,1)S(1)} fusion(bf16[8,2,512,128]{3,2,1,0:T(8,128)(2,1)} %bitcast.72, s32[1024]{0:T(1024)S(1)} %pad_clamp_fusion), kind=kCustom, calls=%fused_computation.2 | custom fusion | bytes 4194336 | tf_op jit(solution)/shard_map/gather | solution.py:42
  103.1 1.5 fusion.44
  104.6 21.3 %reduce-scatter.3.cloned.1.call-done = f32[1,256,256]{1,2,0:T(8,128)} async-done(((f32[8,256,256]{1,2,0:T(8,128)}), f32[1,256,256]{1,2,0:T(8,128)}) %reduce-scatter.3.cloned.1.call-update) | async-done | bytes 262160 | tf_op jit(solution)/shard_map/reduce_scatter | solution.py:67
  125.9 1.0 convert_element_type.21
  126.9 0.0 copy-start.1
  126.9 8.3 %fusion.45 = (f32[256,2]{0,1:T(2,128)S(1)}, bf16[256,2,4096]{2,0,1:T(8,128)(2,1)}) fusion(pred[256,4096]{1,0:T(8,128)(4,1)} %fusion.6, bf16[256,2,128]{0,2,1:T(8,128)(2,1)S(1)} %bitcast.77, bf16[4096,128,1]{1,0,2:T(8,128)(2,1)} %bitcast.75), kind=kOutput, calls=%fused_computation.84 | convolution fusion | flops 549457920 | bytes 6424576 | tf_op jit(solution)/shard_map/sub | solution.py:86
  135.2 0.0 copy-done.1
  135.2 3.7 %fusion.11 = bf16[256,2,128]{0,2,1:T(8,128)(2,1)S(1)} fusion(bf16[4096,128,1]{1,0,2:T(8,128)(2,1)S(1)} %bitcast.71, bf16[256,2,4096]{2,0,1:T(8,128)(2,1)} %get-tuple-element.14, f32[256,2]{0,1:T(2,128)S(1)} %get-tuple-element.13), kind=kOutput, calls=%fused_computation.33 | convolution fusion | flops 537001984 | bytes 5376000 | tf_op jit(solution)/shard_map/nhj,jd->nhd/dot_general | solution.py:88
  138.9 0.8 copy.44
  139.7 0.0 all-gather.2.cloned.1.call-update
  139.7 0.0 reduce-scatter.5.cloned.1.call-start
  139.7 39.4 %all-gather.2.cloned.1.call-done = bf16[8,256,256]{2,1,0:T(8,128)(2,1)} async-done(((bf16[1,256,256]{2,1,0:T(8,128)(2,1)}), bf16[8,256,256]{2,1,0:T(8,128)(2,1)}) %all-gather.2.cloned.1.call-update) | async-done | bytes 1048592 | tf_op jit(solution)/shard_map/all_gather | solution.py:92
  179.1 1.5 copy.45
  180.6 4.4 %fusion.46 = f32[256,1024]{1,0:T(8,128)} fusion(bf16[256,2048]{0,1:T(8,128)(2,1)S(1)} %bitcast.74, bf16[2048,1024]{1,0:T(8,128)(2,1)} %param.13), kind=kOutput, calls=%fused_computation.85 | convolution fusion | flops 1073741824 | bytes 6291456 | tf_op jit(solution)/shard_map/dot_general | solution.py:96
  185.0 0.0 reduce-scatter.5.cloned.1.call-update
  185.0 23.8 %reduce-scatter.5.cloned.1.call-done = f32[64,1024]{1,0:T(8,128)} async-done(((f32[256,1024]{1,0:T(8,128)}), f32[64,1024]{1,0:T(8,128)}) %reduce-scatter.5.cloned.1.call-update) | async-done | bytes 262160 | tf_op jit(solution)/shard_map/reduce_scatter | solution.py:95
  (10 shorter events, 0.2 us)
Async XLA Ops:
  6.5 30.7 %copy-start = (bf16[8,512,128]{2,1,0:T(8,128)(2,1)S(1)}, bf16[8,512,128]{2,1,0:T(8,128)(2,1)}, u32[]{:S(2)}) copy-start(bf16[8,512,128]{2,1,0:T(8,128)(2,1)} %param.12) | copy-start | bytes 3145732
  6.5 119.4 %reduce-scatter.3.cloned.1.call-start = ((), (), s32[]{:S(2)}) async-start(), calls=%async_computation.2 | async-start | bytes 2359296 | tf_op jit(solution)/shard_map/reduce_scatter | solution.py:67
  37.2 141.9 %all-gather.2.cloned.1.call-start = ((), (), s32[]{:S(2)}) async-start(), calls=%async_computation.3 | async-start | bytes 1179648 | tf_op jit(solution)/shard_map/all_gather | solution.py:92
  40.1 8.0 %copy-start.5 = (s32[256]{0:T(256)S(1)}, s32[256]{0:T(256)}, u32[]{:S(2)}) copy-start(s32[256]{0:T(256)} %param.14) | copy-start | bytes 3076
  40.1 8.0 %copy-start.6 = (s32[256]{0:T(256)S(1)}, s32[256]{0:T(256)}, u32[]{:S(2)}) copy-start(s32[256]{0:T(256)} %param.15) | copy-start | bytes 3076
  40.1 57.2 %collective-permute-start.5 = (bf16[1,2,512,128]{3,2,1,0:T(8,128)(2,1)S(1)}, bf16[1,2,512,128]{3,2,1,0:T(8,128)(2,1)}, u32[]{:S(2)}, u32[]{:S(2)}) collective-permute-start(bf16[1,2,512,128]{3,2,1,0:T(8,128)(2,1)S(1)} %fusion.31), channel_id=1, source_target_pairs={{0,24},{4,28},{8,16},{12,20},{16,8},{20,12},{24,0},{28,4},{1,25},{... | collective-permute-start | bytes 786440 | tf_op jit(solution)/shard_map/ppermute | solution.py:39
  41.4 56.9 %collective-permute-start.6 = (bf16[1,2,512,128]{3,2,0,1:T(8,128)(2,1)}, bf16[1,2,512,128]{3,2,0,1:T(8,128)(2,1)}, u32[]{:S(2)}, u32[]{:S(2)}) collective-permute-start(bf16[1,2,512,128]{3,2,0,1:T(8,128)(2,1)} %get-tuple-element.7), channel_id=1, source_target_pairs={{0,28},{4,24},{8,20},{12,16},{16,12},{20,8},{24,4},{28,0},{1,29},{... | collective-permute-start | bytes 786440 | tf_op jit(solution)/shard_map/ppermute | solution.py:39
  42.4 14.5 %collective-permute-start = (bf16[1,2,512,128]{3,2,1,0:T(8,128)(2,1)}, bf16[1,2,512,128]{3,2,1,0:T(8,128)(2,1)}, u32[]{:S(2)}, u32[]{:S(2)}) collective-permute-start(bf16[1,2,512,128]{3,2,1,0:T(8,128)(2,1)} %get-tuple-element.8), channel_id=1, source_target_pairs={{0,4},{4,0},{8,12},{12,8},{16,20},{20,16},{24,28},{28,24},{1,5},{5... | collective-permute-start | bytes 786440 | tf_op jit(solution)/shard_map/ppermute | solution.py:39
  46.6 27.4 %collective-permute-start.1 = (bf16[1,2,512,128]{3,2,1,0:T(8,128)(2,1)}, bf16[1,2,512,128]{3,2,1,0:T(8,128)(2,1)}, u32[]{:S(2)}, u32[]{:S(2)}) collective-permute-start(bf16[1,2,512,128]{3,2,1,0:T(8,128)(2,1)} %get-tuple-element.9), channel_id=1, source_target_pairs={{0,8},{4,12},{8,0},{12,4},{16,24},{20,28},{24,16},{28,20},{1,9},{5... | collective-permute-start | bytes 786440 | tf_op jit(solution)/shard_map/ppermute | solution.py:39
  46.6 37.7 %collective-permute-start.2 = (bf16[1,2,512,128]{3,2,1,0:T(8,128)(2,1)}, bf16[1,2,512,128]{3,2,1,0:T(8,128)(2,1)}, u32[]{:S(2)}, u32[]{:S(2)}) collective-permute-start(bf16[1,2,512,128]{3,2,1,0:T(8,128)(2,1)} %get-tuple-element.10), channel_id=1, source_target_pairs={{0,12},{4,8},{8,4},{12,0},{16,28},{20,24},{24,20},{28,16},{1,13},{... | collective-permute-start | bytes 786440 | tf_op jit(solution)/shard_map/ppermute | solution.py:39
  50.0 7.0 %copy-start.4 = (bf16[1,2,512,128]{3,2,1,0:T(8,128)(2,1)S(1)}, bf16[1,2,512,128]{3,2,1,0:T(8,128)(2,1)}, u32[]{:S(2)}) copy-start(bf16[1,2,512,128]{3,2,1,0:T(8,128)(2,1)} %get-tuple-element.11) | copy-start | bytes 786436
  50.0 24.1 %copy-start.3 = (bf16[1,2,512,128]{3,2,1,0:T(8,128)(2,1)S(1)}, bf16[1,2,512,128]{3,2,1,0:T(8,128)(2,1)}, u32[]{:S(2)}) copy-start(bf16[1,2,512,128]{3,2,1,0:T(8,128)(2,1)} %get-tuple-element.12) | copy-start | bytes 786436
  57.0 39.2 %collective-permute-start.3 = (bf16[1,2,512,128]{3,2,1,0:T(8,128)(2,1)S(1)}, bf16[1,2,512,128]{3,2,1,0:T(8,128)(2,1)S(1)}, u32[]{:S(2)}, u32[]{:S(2)}) collective-permute-start(bf16[1,2,512,128]{3,2,1,0:T(8,128)(2,1)S(1)} %copy-done.4), channel_id=1, source_target_pairs={{0,16},{4,20},{8,24},{12,28},{16,0},{20,4},{24,8},{28,12},{1,17},{... | collective-permute-start | bytes 786440 | tf_op jit(solution)/shard_map/ppermute | solution.py:39
  74.0 23.2 %collective-permute-start.4 = (bf16[1,2,512,128]{3,2,1,0:T(8,128)(2,1)S(1)}, bf16[1,2,512,128]{3,2,1,0:T(8,128)(2,1)S(1)}, u32[]{:S(2)}, u32[]{:S(2)}) collective-permute-start(bf16[1,2,512,128]{3,2,1,0:T(8,128)(2,1)S(1)} %copy-done.3), channel_id=1, source_target_pairs={{0,20},{4,16},{8,28},{12,24},{16,4},{20,0},{24,12},{28,8},{1,21},{... | collective-permute-start | bytes 786440 | tf_op jit(solution)/shard_map/ppermute | solution.py:39
  99.2 1.3 copy-start.2
  126.9 8.3 %copy-start.1 = (bf16[1,8,512,128]{3,2,0,1:T(8,128)(2,1)S(1)}, bf16[1,8,512,128]{3,2,0,1:T(8,128)(2,1)}, u32[]{:S(2)}) copy-start(bf16[1,8,512,128]{3,2,0,1:T(8,128)(2,1)} %get-tuple-element.6) | copy-start | bytes 3145732
  139.7 69.2 %reduce-scatter.5.cloned.1.call-start = ((), (), s32[]{:S(2)}) async-start(), calls=%async_computation.4 | async-start | bytes 1310720 | tf_op jit(solution)/shard_map/reduce_scatter | solution.py:95
Sparse Core Ops, SparseCore 0:
  37.3 88.5 reduce-scatter.2
  139.8 39.2 all-gather.1
  185.2 23.6 reduce-scatter.4
